TPU v7x, 32 devices: a whole 2x2x4 slice. The times are simulated.
32 devices in a mesh: dp: 16 (over z, y, x), tensor: 2 (over core).
Axes of the slice: x: 2, y: 2, z: 4, core: 2. Of those that a mesh axis runs over, the one named last changes fastest.
Arguments:
- block_input: bfloat16 [3136, 512], P('dp'), may hold values from -6 to 6
- ln1_gain: float32 [512], replicated, may hold values from 0.1 to 1.9
- ln1_bias: float32 [512], replicated, may hold values from -3 to 3
- w_qkv: bfloat16 [3, 512, 512], P(None, None, 'tensor'), may hold values from -0.25 to 0.25
- qv_bias: float32 [2, 512], P(None, 'tensor'), may hold values from -3 to 3
- bias_table: float32 [169, 16], P(None, 'tensor'), may hold values from -4 to 4
- w_proj: bfloat16 [512, 512], P('tensor'), may hold values from -1 to 1
- proj_bias: float32 [512], replicated, may hold values from -3 to 3
- ln2_gain: float32 [512], replicated, may hold values from 0.1 to 1.9
- ln2_bias: float32 [512], replicated, may hold values from -3 to 3
- w_fc1: bfloat16 [512, 2048], P(None, 'tensor'), may hold values from -0.25 to 0.25
- fc1_bias: float32 [2048], P('tensor'), may hold values from -3 to 3
- w_fc2: bfloat16 [2048, 512], P('tensor'), may hold values from -0.1875 to 0.1875
- fc2_bias: float32 [512], replicated, may hold values from -3 to 3
- region_ids: int32 [4, 49], replicated, may hold values from 0 to 3
- rel_index: int32 [49, 49], replicated, may hold values from 0 to 168
- cotangent: bfloat16 [3136, 512], P('dp'), may hold values from -6 to 6
Outputs:
- block_output: float32 [3136, 512], P('dp')
- dx: float32 [3136, 512], P('dp')
- g_ln1_gain: float32 [512], replicated
- g_ln1_bias: float32 [512], replicated
- g_qkv: float32 [3, 512, 512], P(None, None, 'tensor')
- g_qv_bias: float32 [2, 512], P(None, 'tensor')
- g_table: float32 [169, 16], P(None, 'tensor')
- g_proj: float32 [512, 512], P('tensor')
- g_proj_bias: float32 [512], replicated
- g_ln2_gain: float32 [512], replicated
- g_ln2_bias: float32 [512], replicated
- g_fc1: float32 [512, 2048], P(None, 'tensor')
- g_fc1_bias: float32 [2048], P('tensor')
- g_fc2: float32 [2048, 512], P('tensor')
- g_fc2_bias: float32 [512], replicated
All inputs are finite; a program needn't handle non-finite values.
Results may differ from a plain program's by a relative error of at most 0.012.
Values sent between devices are 32-bit elements; how exact they have to be, the bound alone decides.
No kernel may reach another device: no remote copies, remote signals or barrier semaphores. Data moves between devices by JAX's collectives and lax.ppermute only.
A program may use at most 64 MiB of HBM per device.

v0:
```python
import jax
import jax.numpy as jnp
from jax import lax
from jax.sharding import PartitionSpec as P

SIDE = 14
WIN = 7
SHIFT = 3
NWIN = 4
WTOK = 49
TABLE = 169


def layer_stats(values, gain, bias):
    mean = jnp.mean(values, -1, keepdims=True)
    centred = values - mean
    var = jnp.mean(centred * centred, -1, keepdims=True)
    rstd = lax.rsqrt(var + 1e-05)
    nhat = centred * rstd
    return (nhat * gain + bias, nhat, rstd)


def layer_back(dout, nhat, rstd, gain):
    dnorm = dout * gain
    return rstd * (
        dnorm
        - jnp.mean(dnorm, -1, keepdims=True)
        - nhat * jnp.mean(dnorm * nhat, -1, keepdims=True)
    )


def to_windows(values, nimg):
    width = values.shape[-1]
    per = SIDE // WIN
    grid = values.reshape(nimg, SIDE, SIDE, width)
    grid = jnp.roll(grid, (-SHIFT, -SHIFT), (1, 2))
    grid = grid.reshape(nimg, per, WIN, per, WIN, width).transpose(0, 1, 3, 2, 4, 5)
    return grid.reshape(-1, width)


def from_windows(values, nimg):
    width = values.shape[-1]
    per = SIDE // WIN
    grid = values.reshape(nimg, per, per, WIN, WIN, width).transpose(0, 1, 3, 2, 4, 5)
    grid = grid.reshape(nimg, SIDE, SIDE, width)
    grid = jnp.roll(grid, (SHIFT, SHIFT), (1, 2))
    return grid.reshape(-1, width)


def gelu_value(u):
    return 0.5 * u * (1.0 + lax.erf(u * 0.7071067811865476))


def gelu_slope(u):
    return (
        0.5 * (1.0 + lax.erf(u * 0.7071067811865476))
        + u * jnp.exp(-0.5 * u * u) * 0.3989422804014327
    )


def inner(left, right):
    return lax.dot_general(
        left, right, (((0,), (0,)), ((), ())), preferred_element_type=jnp.float32
    )


def outer(left, right):
    return lax.dot_general(
        left, right, (((1,), (1,)), ((), ())), preferred_element_type=jnp.float32
    )


def mixed(form, left, right):
    return jnp.einsum(form, left, right, preferred_element_type=jnp.float32)


def body(
    block_input,
    ln1_gain,
    ln1_bias,
    w_qkv,
    qv_bias,
    bias_table,
    w_proj,
    proj_bias,
    ln2_gain,
    ln2_bias,
    w_fc1,
    fc1_bias,
    w_fc2,
    fc2_bias,
    region_ids,
    rel_index,
    cotangent,
):
    nimg = block_input.shape[0] // (SIDE * SIDE)
    heads = bias_table.shape[1]
    local_width = w_qkv.shape[2]
    hdim = local_width // heads
    scale = hdim ** (-0.5)
    shape5 = (nimg, NWIN, WTOK, heads, hdim)
    onehot = (rel_index.reshape(-1)[:, None] == lax.iota(jnp.int32, TABLE)[None, :]).astype(
        jnp.float32
    )
    bias = jnp.dot(onehot, bias_table, precision=lax.Precision.HIGHEST).T.reshape(heads, WTOK, WTOK)
    same = region_ids[:, :, None] == region_ids[:, None, :]
    mask = jnp.where(same, jnp.float32(0.0), jnp.float32(-100.0))
    xf = block_input.astype(jnp.float32)
    anorm, nhat1, rstd1 = layer_stats(xf, ln1_gain, ln1_bias)
    aw = to_windows(anorm.astype(jnp.bfloat16), nimg)
    query = (
        (jnp.dot(aw, w_qkv[0], preferred_element_type=jnp.float32) + qv_bias[0]) * scale
    ).astype(jnp.bfloat16)
    keys = jnp.dot(aw, w_qkv[1], preferred_element_type=jnp.float32).astype(jnp.bfloat16)
    values = (jnp.dot(aw, w_qkv[2], preferred_element_type=jnp.float32) + qv_bias[1]).astype(
        jnp.bfloat16
    )
    q5 = query.reshape(shape5)
    k5 = keys.reshape(shape5)
    v5 = values.reshape(shape5)
    scores = mixed("nwihd,nwjhd->nwhij", q5, k5) + bias[None, None] + mask[None, :, None]
    expo = jnp.exp(scores)
    total = jnp.sum(expo, -1, keepdims=True)
    probs = expo / total
    lse = jnp.log(total)
    attn5 = mixed("nwhij,nwjhd->nwihd", probs.astype(jnp.bfloat16), v5).astype(jnp.bfloat16)
    attn_flat = attn5.reshape(-1, local_width)
    projected = lax.psum(jnp.dot(attn_flat, w_proj, preferred_element_type=jnp.float32), "tensor")
    hres = xf + from_windows(projected, nimg) + proj_bias
    cnorm, nhat2, rstd2 = layer_stats(hres, ln2_gain, ln2_bias)
    cb = cnorm.astype(jnp.bfloat16)
    upre = jnp.dot(cb, w_fc1, preferred_element_type=jnp.float32) + fc1_bias
    zact = gelu_value(upre).astype(jnp.bfloat16)
    mlp_out = lax.psum(jnp.dot(zact, w_fc2, preferred_element_type=jnp.float32), "tensor")
    block_output = hres + mlp_out + fc2_bias
    gf = cotangent.astype(jnp.float32)
    g_fc2_bias = jnp.sum(gf, 0)
    g_fc2 = inner(zact, cotangent)
    du = outer(cotangent, w_fc2) * gelu_slope(upre)
    g_fc1_bias = jnp.sum(du, 0)
    dub = du.astype(jnp.bfloat16)
    g_fc1 = inner(cb, dub)
    dcn = lax.psum(outer(dub, w_fc1), "tensor")
    g_ln2_gain = jnp.sum(dcn * nhat2, 0)
    g_ln2_bias = jnp.sum(dcn, 0)
    dh = gf + layer_back(dcn, nhat2, rstd2, ln2_gain)
    g_proj_bias = jnp.sum(dh, 0)
    dhw = to_windows(dh, nimg).astype(jnp.bfloat16)
    g_proj = inner(attn_flat, dhw)
    dout = outer(dhw, w_proj).astype(jnp.bfloat16)
    d5 = dout.reshape(shape5)
    scores = mixed("nwihd,nwjhd->nwhij", q5, k5) + bias[None, None] + mask[None, :, None]
    probs = jnp.exp(scores - lse)
    pb = probs.astype(jnp.bfloat16)
    dprob = mixed("nwihd,nwjhd->nwhij", d5, v5)
    delta = jnp.sum(d5.astype(jnp.float32) * attn5.astype(jnp.float32), -1).transpose(0, 1, 3, 2)[
        ..., None
    ]
    dscore = probs * (dprob - delta)
    dv = mixed("nwhij,nwihd->nwjhd", pb, d5).reshape(-1, local_width)
    dbias = jnp.sum(dscore, (0, 1)).reshape(heads, WTOK * WTOK)
    g_table = lax.dot_general(
        onehot, dbias, (((0,), (1,)), ((), ())), precision=lax.Precision.HIGHEST
    )
    dsb = dscore.astype(jnp.bfloat16)
    dq = (mixed("nwhij,nwjhd->nwihd", dsb, k5) * scale).reshape(-1, local_width)
    dk = mixed("nwhij,nwihd->nwjhd", dsb, q5).reshape(-1, local_width)
    g_qv_bias = jnp.stack([jnp.sum(dq, 0), jnp.sum(dv, 0)])
    dqb = dq.astype(jnp.bfloat16)
    dkb = dk.astype(jnp.bfloat16)
    dvb = dv.astype(jnp.bfloat16)
    g_qkv = jnp.stack([inner(aw, dqb), inner(aw, dkb), inner(aw, dvb)])
    daw = outer(dqb, w_qkv[0]) + outer(dkb, w_qkv[1]) + outer(dvb, w_qkv[2])
    dan = lax.psum(from_windows(daw, nimg), "tensor")
    g_ln1_gain = jnp.sum(dan * nhat1, 0)
    g_ln1_bias = jnp.sum(dan, 0)
    dx = dh + layer_back(dan, nhat1, rstd1, ln1_gain)
    (
        g_ln1_gain,
        g_ln1_bias,
        g_qkv,
        g_qv_bias,
        g_table,
        g_proj,
        g_proj_bias,
        g_ln2_gain,
        g_ln2_bias,
        g_fc1,
        g_fc1_bias,
        g_fc2,
        g_fc2_bias,
    ) = lax.psum(
        (
            g_ln1_gain,
            g_ln1_bias,
            g_qkv,
            g_qv_bias,
            g_table,
            g_proj,
            g_proj_bias,
            g_ln2_gain,
            g_ln2_bias,
            g_fc1,
            g_fc1_bias,
            g_fc2,
            g_fc2_bias,
        ),
        "dp",
    )
    return (
        block_output,
        dx,
        g_ln1_gain,
        g_ln1_bias,
        g_qkv,
        g_qv_bias,
        g_table,
        g_proj,
        g_proj_bias,
        g_ln2_gain,
        g_ln2_bias,
        g_fc1,
        g_fc1_bias,
        g_fc2,
        g_fc2_bias,
    )


def solution(mesh):
    return jax.shard_map(
        body,
        mesh=mesh,
        in_specs=(
            P("dp", None),
            P(),
            P(),
            P(None, None, "tensor"),
            P(None, "tensor"),
            P(None, "tensor"),
            P("tensor", None),
            P(),
            P(),
            P(),
            P(None, "tensor"),
            P("tensor"),
            P("tensor", None),
            P(),
            P(),
            P(),
            P("dp", None),
        ),
        out_specs=(
            P("dp", None),
            P("dp", None),
            P(),
            P(),
            P(None, None, "tensor"),
            P(None, "tensor"),
            P(None, "tensor"),
            P("tensor", None),
            P(),
            P(),
            P(),
            P(None, "tensor"),
            P("tensor"),
            P("tensor", None),
            P(),
        ),
        check_vma=False,
    )
```

profile of v0, /device:TPU:0, one launch (start us, length us, event | category | flops | bytes accessed | tf_op | source)
XLA Modules:
  0.0 377.0 jit_solution(15921145427322588425)
XLA Ops:
  13.9 1.9 convolution_bitcast_fusion
  27.3 2.2 copy.85
  29.6 21.2 %all-reduce.8.cloned.1.call-done = f32[1,14,14,512]{3,0,2,1:T(1,128)} async-done(((f32[1,14,14,512]{3,0,2,1:T(1,128)}), f32[1,14,14,512]{3,0,2,1:T(1,128)}) %all-reduce.8.cloned.1.call-update) | async-done | bytes 401424 | tf_op jit(solution)/shard_map/psum | solution.py:128
  52.9 1.8 fusion.38
  60.6 2.4 fusion.68
  63.0 1.9 fusion.55
  64.9 15.3 %all-reduce.10.cloned.1.call-done = f32[196,512]{1,0:T(8,128)} async-done(((f32[196,512]{1,0:T(8,128)}), f32[196,512]{1,0:T(8,128)}) %all-reduce.10.cloned.1.call-update) | async-done | bytes 401424 | tf_op jit(solution)/shard_map/psum | solution.py:143
  80.2 1.9 multiply_reduce_fusion.1
  82.0 2.6 fusion.59
  84.7 1.7 reshape.241
  92.3 1.7 convert_element_type.127
  94.0 1.9 convolution_convert_fusion.2
  95.9 1.9 reshape.252
  97.8 2.0 reshape.248
  99.9 2.0 copy.88
  101.8 2.3 copy.91
  112.1 1.9 copy.98
  115.1 1.9 copy.95
  122.6 1.8 fusion.70
  129.7 13.3 %all-reduce.14.cloned.1.call-done = (f32[196,512]{1,0:T(8,128)}, f32[196,512]{1,0:T(8,128)}) async-done(((f32[196,512]{1,0:T(8,128)}, f32[196,512]{1,0:T(8,128)}), (f32[196,512]{1,0:T(8,128)}, f32[196,512]{1,0:T(8,128)})) %all-reduce.14.cloned.1.call-update) | async-done | bytes 802832 | tf_op jit(solution)/shard_map/psum | solution.py:134
  144.5 80.1 %all-reduce = (f32[512]{0:T(512)}, f32[512]{0:T(512)}, f32[2,256]{1,0:T(2,128)}, f32[169,8]{0,1:T(8,128)}, f32[512]{0:T(512)}, /*index=5*/f32[512]{0:T(512)}, f32[512]{0:T(512)}, f32[1024]{0:T(1024)}, f32[512]{0:T(512)}) all-reduce(f32[512]{0:T(512)S(1)} %get-tuple-element.17, ...), channel_id=1, replica_groups=mesh['dp'=16,'tensor'=2] {'dp'}, use_global_device_ids=true, to_apply=%region_15.16 | all-reduce | flops 5960 | bytes 47680 | tf_op jit(solution)/shard_map/psum | solution.py:192
  224.5 1.8 add_add_fusion
  227.3 135.8 %all-reduce.12.cloned.1.call-done = (f32[3,512,256]{2,1,0:T(8,128)}, f32[256,512]{1,0:T(8,128)}, f32[512,1024]{1,0:T(8,128)}, f32[1024,512]{1,0:T(8,128)}) async-done(((f32[3,512,256]{2,1,0:T(8,128)}, f32[256,512]{1,0:T(8,128)}, f32[512,1024]{1,0:T(8,128)}, f32[1024,512]{1,0:T(8,128)}), (f32[3,512,256]{2,1,0:T(8,128)}, f32[256,512]{1,0:T(8,128)}, f32[512,1024]{1,0:T(8,128)}, ...) | async-done | bytes 6291472 | tf_op jit(solution)/shard_map/psum | solution.py:192
  363.1 2.8 copy.129
  (171 shorter events, 58.3 us)
Async XLA Ops:
  7.2 49.1 %copy-start = (bf16[512,1024]{1,0:T(8,128)(2,1)S(1)}, bf16[512,1024]{1,0:T(8,128)(2,1)}, u32[]{:S(2)}) copy-start(bf16[512,1024]{1,0:T(8,128)(2,1)} %param.27) | copy-start | bytes 3145732
  7.2 43.6 %all-reduce.8.cloned.1.call-start = ((), (), s32[]{:S(2)}) async-start(), calls=%async_computation | async-start | bytes 802816 | tf_op jit(solution)/shard_map/psum | solution.py:128
  10.8 6.4 %copy-start.12 = (bf16[3,512,256]{2,1,0:T(8,128)(2,1)S(1)}, bf16[3,512,256]{2,1,0:T(8,128)(2,1)}, u32[]{:S(2)}) copy-start(bf16[3,512,256]{2,1,0:T(8,128)(2,1)} %param.20) | copy-start | bytes 2359300
  21.7 4.1 %copy-start.17 = (bf16[256,512]{1,0:T(8,128)(2,1)S(1)}, bf16[256,512]{1,0:T(8,128)(2,1)}, u32[]{:S(2)}) copy-start(bf16[256,512]{1,0:T(8,128)(2,1)} %param.23) | copy-start | bytes 786436
  27.3 28.5 %copy-start.1 = (bf16[196,512]{1,0:T(8,128)(2,1)S(1)}, bf16[196,512]{1,0:T(8,128)(2,1)}, u32[]{:S(2)}) copy-start(bf16[196,512]{1,0:T(8,128)(2,1)} %param.17) | copy-start | bytes 602116
  27.3 28.5 %copy-start.36 = (f32[512]{0:T(512)S(1)}, f32[512]{0:T(512)}, u32[]{:S(2)}) copy-start(f32[512]{0:T(512)} %param.24) | copy-start | bytes 6148
  29.5 26.7 %copy-start.25 = (f32[512]{0:T(512)S(1)}, f32[512]{0:T(512)}, u32[]{:S(2)}) copy-start(f32[512]{0:T(512)} %param.25) | copy-start | bytes 6148
  29.6 26.7 %copy-start.29 = (f32[512]{0:T(512)S(1)}, f32[512]{0:T(512)}, u32[]{:S(2)}) copy-start(f32[512]{0:T(512)} %param.26) | copy-start | bytes 6148
  29.6 26.7 %copy-start.34 = (f32[1024]{0:T(1024)S(1)}, f32[1024]{0:T(1024)}, u32[]{:S(2)}) copy-start(f32[1024]{0:T(1024)} %param.28) | copy-start | bytes 12292
  29.6 50.6 %all-reduce.10.cloned.1.call-start = ((), (), s32[]{:S(2)}) async-start(), calls=%async_computation.1 | async-start | bytes 819200 | tf_op jit(solution)/shard_map/psum | solution.py:143
  60.3 82.7 %all-reduce.14.cloned.1.call-start = ((), (), s32[]{:S(2)}) async-start(), calls=%async_computation.3 | async-start | bytes 1638400 | tf_op jit(solution)/shard_map/psum | solution.py:134
  104.1 3.9 %copy-start.4 = (bf16[4,49,8,32]{1,3,2,0:T(8,128)(2,1)S(1)}, bf16[4,49,8,32]{1,3,2,0:T(8,128)(2,1)}, u32[]{:S(2)}) copy-start(bf16[4,49,8,32]{1,3,2,0:T(8,128)(2,1)} %copy-done.3) | copy-start | bytes 301060
  109.0 9.1 %copy-start.13 = (bf16[3,512,256]{2,1,0:T(8,128)(2,1)S(1)}, bf16[3,512,256]{2,1,0:T(8,128)(2,1)}, u32[]{:S(2)}) copy-start(bf16[3,512,256]{2,1,0:T(8,128)(2,1)} %param.20) | copy-start | bytes 2359300
  122.5 240.6 %all-reduce.12.cloned.1.call-start = ((), (), s32[]{:S(2)}) async-start(), calls=%async_computation.2 | async-start | bytes 12582912 | tf_op jit(solution)/shard_map/psum | solution.py:192
  127.5 15.5 %copy-start.26 = (f32[512]{0:T(512)S(1)}, f32[512]{0:T(512)}, u32[]{:S(2)}) copy-start(f32[512]{0:T(512)} %param.18) | copy-start | bytes 6148
  127.5 16.9 %copy-start.30 = (f32[512]{0:T(512)S(1)}, f32[512]{0:T(512)}, u32[]{:S(2)}) copy-start(f32[512]{0:T(512)} %get-tuple-element.15) | copy-start | bytes 6148
  127.5 16.9 %copy-start.31 = (f32[512]{0:T(512)S(1)}, f32[512]{0:T(512)}, u32[]{:S(2)}) copy-start(f32[512]{0:T(512)} %get-tuple-element.21) | copy-start | bytes 6148
  127.5 16.9 %copy-start.32 = (f32[512]{0:T(512)S(1)}, f32[512]{0:T(512)}, u32[]{:S(2)}) copy-start(f32[512]{0:T(512)} %get-tuple-element.38) | copy-start | bytes 6148
  127.5 16.9 %copy-start.33 = (f32[512]{0:T(512)S(1)}, f32[512]{0:T(512)}, u32[]{:S(2)}) copy-start(f32[512]{0:T(512)} %get-tuple-element.46) | copy-start | bytes 6148
  127.6 16.9 %copy-start.35 = (f32[1024]{0:T(1024)S(1)}, f32[1024]{0:T(1024)}, u32[]{:S(2)}) copy-start(f32[1024]{0:T(1024)} %get-tuple-element.57) | copy-start | bytes 12292
  127.6 96.9 %copy-start.37 = (f32[512]{0:T(512)S(1)}, f32[512]{0:T(512)}, u32[]{:S(2)}) copy-start(f32[512]{0:T(512)} %param.30) | copy-start | bytes 6148
  127.6 98.7 %copy-start.2 = (f32[196,512]{1,0:T(8,128)S(1)}, f32[196,512]{1,0:T(8,128)}, u32[]{:S(2)}) copy-start(f32[196,512]{1,0:T(8,128)} %get-tuple-element.39) | copy-start | bytes 1204228
  143.0 83.3 %copy-start.11 = (f32[196,512]{1,0:T(8,128)S(1)}, f32[196,512]{1,0:T(8,128)}, u32[]{:S(2)}) copy-start(f32[196,512]{1,0:T(8,128)} %get-tuple-element.37) | copy-start | bytes 1204228
  363.1 3.6 copy-start.7
  (18 other events, 32.5 us)
Sparse Core Ops, SparseCore 0:
  29.7 21.1 all-reduce.7
  60.5 19.6 all-reduce.9
  122.6 20.3 all-reduce.13
  150.5 212.6 all-reduce.11
where the time goes:
time: 378 us; the launch traced here: 377 us
  waiting for transfers between devices  186 us (49%)
  blocking collectives  80.1 us (21%)
  local copies, waits for them, and re-layouts  50.5 us (13%)
  matrix products  25.6 us (7%)
  other arithmetic  20.3 us (5%)
  between operations  14.5 us (4%)
    psum x1, waiting for transfers between devices, body(): lax.psum((g_ln1_gain, g_ln1_bias, g_qkv, g_qv_bias, g_table, g_proj, g_pr...  136 us
    psum x1, blocking collectives, body(): lax.psum((g_ln1_gain, g_ln1_bias, g_qkv, g_qv_bias, g_table, g_proj, g_pr...  80.1 us
    psum x1, waiting for transfers between devices, body(): lax.psum(jnp.dot(attn_flat, w_proj, preferred_element_type=jnp.float32),...  21.2 us
    psum x1, waiting for transfers between devices, body(): dcn = lax.psum(outer(dub, w_fc1), 'tensor')  15.3 us
    psum x1, waiting for transfers between devices, body(): lax.psum(jnp.dot(zact, w_fc2, preferred_element_type=jnp.float32), 'tensor')  13.3 us
    unnamed x80, local copies, waits for them, and re-layouts  10.4 us
  transfers between devices with their start and end apart: 4, of which 4 were waited for; matrix products, arithmetic and copies ran while one was open for 4% of the time, Pallas kernels for 0%

commit v1 on v0

--- a/solution.py
+++ b/solution.py
@@ -131,7 +131,9 @@
     cb = cnorm.astype(jnp.bfloat16)
     upre = jnp.dot(cb, w_fc1, preferred_element_type=jnp.float32) + fc1_bias
     zact = gelu_value(upre).astype(jnp.bfloat16)
-    mlp_out = lax.psum(jnp.dot(zact, w_fc2, preferred_element_type=jnp.float32), "tensor")
+    mlp_out = jnp.sum(
+        lax.all_gather(jnp.dot(zact, w_fc2, preferred_element_type=jnp.float32), "tensor"), axis=0
+    )
     block_output = hres + mlp_out + fc2_bias
     gf = cotangent.astype(jnp.float32)
     g_fc2_bias = jnp.sum(gf, 0)

time: 378 us -> 364 us (0.963)
  local copies, waits for them, and re-layouts: 50.5 us -> 34.9 us
  blocking collectives: 80.1 us -> 87 us
  waiting for transfers between devices: 186 us -> 181 us
    all_gather x0 -> x1, blocking collectives: none -> 6.94 us  [body(): lax.all_gather(jnp.dot(zact, w_fc2, preferred_element_type=jnp.float32),...]
    psum x1, waiting for transfers between devices: 15.3 us -> 8.93 us  [body(): dcn = lax.psum(outer(dub, w_fc1), 'tensor')]
    unnamed x80 -> x76, local copies, waits for them, and re-layouts: 10.4 us -> 9.93 us
  transfers between devices with their start and end apart: 4 -> 4, of which waited for: 4 -> 4; matrix products, arithmetic and copies ran while one was open for 4% -> 3% of each run, Pallas kernels for 0% -> 0%
where the time goes in v1:
time: 364 us; the launch traced here: 363 us
  waiting for transfers between devices  181 us (50%)
  blocking collectives  87 us (24%)
  local copies, waits for them, and re-layouts  34.9 us (10%)
  matrix products  23.8 us (7%)
  other arithmetic  21.7 us (6%)
  between operations  14.5 us (4%)
    psum x1, waiting for transfers between devices, body(): lax.psum((g_ln1_gain, g_ln1_bias, g_qkv, g_qv_bias, g_table, g_proj, g_pr...  137 us
    psum x1, blocking collectives, body(): lax.psum((g_ln1_gain, g_ln1_bias, g_qkv, g_qv_bias, g_table, g_proj, g_pr...  80 us
    psum x1, waiting for transfers between devices, body(): lax.psum(jnp.dot(attn_flat, w_proj, preferred_element_type=jnp.float32),...  21.2 us
    psum x1, waiting for transfers between devices, body(): dan = lax.psum(from_windows(daw, nimg), 'tensor')  14.1 us
    unnamed x76, local copies, waits for them, and re-layouts  9.93 us
    psum x1, waiting for transfers between devices, body(): dcn = lax.psum(outer(dub, w_fc1), 'tensor')  8.93 us
    dot_general x6, matrix products, inner(): lax.dot_general(left, right, (((0,), (0,)), ((), ())), preferred_element_...  7.37 us
  transfers between devices with their start and end apart: 4, of which 4 were waited for; matrix products, arithmetic and copies ran while one was open for 3% of the time, Pallas kernels for 0%

profile of v1, /device:TPU:0, one launch (start us, length us, event | category | flops | bytes accessed | tf_op | source)
XLA Modules:
  0.0 363.1 jit_solution(11654969663080202707)
XLA Ops:
  13.3 1.9 convolution_bitcast_fusion
  19.4 1.3 fusion.6
  25.5 21.2 %all-reduce.7.cloned.1.call-done = f32[1,14,14,512]{3,0,2,1:T(1,128)} async-done(((f32[1,14,14,512]{3,0,2,1:T(1,128)}), f32[1,14,14,512]{3,0,2,1:T(1,128)}) %all-reduce.7.cloned.1.call-update) | async-done | bytes 401424 | tf_op jit(solution)/shard_map/psum | solution.py:128
  52.8 1.8 fusion.69
  57.1 6.9 %all-gather.1 = f32[2,196,512]{2,1,0:T(8,128)} all-gather(f32[1,196,512]{2,1,0:T(8,128)} %convolution_bitcast_fusion.5), channel_id=2, replica_groups=mesh['dp'=16,'tensor'=2] {'tensor'}, dimensions={0}, use_global_device_ids=true | all-gather | bytes 1204224 | tf_op jit(solution)/shard_map/all_gather | solution.py:135
  64.0 2.0 reduce_sum.196
  66.0 1.9 fusion.55
  68.0 8.9 %all-reduce.9.cloned.1.call-done = f32[196,512]{1,0:T(8,128)} async-done(((f32[196,512]{1,0:T(8,128)}), f32[196,512]{1,0:T(8,128)}) %all-reduce.9.cloned.1.call-update) | async-done | bytes 401424 | tf_op jit(solution)/shard_map/psum | solution.py:145
  76.9 1.9 multiply_reduce_fusion.1
  78.8 2.8 fusion.59
  86.1 1.9 reshape.256
  88.0 2.0 reshape.252
  90.0 1.3 copy.88
  91.3 2.3 copy.91
  105.7 1.8 fusion.36
  107.5 1.8 reshape.245
  115.1 14.1 %all-reduce.11.cloned.1.call-done = f32[196,512]{1,0:T(8,128)} async-done(((f32[196,512]{1,0:T(8,128)}), f32[196,512]{1,0:T(8,128)}) %all-reduce.11.cloned.1.call-update) | async-done | bytes 401424 | tf_op jit(solution)/shard_map/psum | solution.py:176
  129.2 1.3 fusion.32
  130.5 80.0 %all-reduce = (f32[512]{0:T(512)}, f32[512]{0:T(512)}, f32[2,256]{1,0:T(2,128)}, f32[169,8]{0,1:T(8,128)}, f32[512]{0:T(512)}, /*index=5*/f32[512]{0:T(512)}, f32[512]{0:T(512)}, f32[1024]{0:T(1024)}, f32[512]{0:T(512)}) all-reduce(f32[512]{0:T(512)S(1)} %get-tuple-element.17, ...), channel_id=1, replica_groups=mesh['dp'=16,'tensor'=2] {'dp'}, use_global_device_ids=true, to_apply=%region_15.16 | all-reduce | flops 5960 | bytes 47680 | tf_op jit(solution)/shard_map/psum | solution.py:194
  210.5 1.9 fusion.31
  212.5 136.8 %all-reduce.13.cloned.1.call-done = (f32[3,512,256]{2,1,0:T(8,128)}, f32[256,512]{1,0:T(8,128)}, f32[512,1024]{1,0:T(8,128)}, f32[1024,512]{1,0:T(8,128)}) async-done(((f32[3,512,256]{2,1,0:T(8,128)}, f32[256,512]{1,0:T(8,128)}, f32[512,1024]{1,0:T(8,128)}, f32[1024,512]{1,0:T(8,128)}), (f32[3,512,256]{2,1,0:T(8,128)}, f32[256,512]{1,0:T(8,128)}, f32[512,1024]{1,0:T(8,128)}, ...) | async-done | bytes 6291472 | tf_op jit(solution)/shard_map/psum | solution.py:194
  349.3 2.8 copy.128
  352.9 1.3 copy.130
  355.2 1.3 copy.131
  (168 shorter events, 47.1 us)
Async XLA Ops:
  7.2 43.9 %copy-start = (bf16[512,1024]{1,0:T(8,128)(2,1)S(1)}, bf16[512,1024]{1,0:T(8,128)(2,1)}, u32[]{:S(2)}) copy-start(bf16[512,1024]{1,0:T(8,128)(2,1)} %param.27) | copy-start | bytes 3145732
  7.2 39.5 %all-reduce.7.cloned.1.call-start = ((), (), s32[]{:S(2)}) async-start(), calls=%async_computation | async-start | bytes 802816 | tf_op jit(solution)/shard_map/psum | solution.py:128
  10.8 5.1 %copy-start.6 = (bf16[3,512,256]{2,1,0:T(8,128)(2,1)S(1)}, bf16[3,512,256]{2,1,0:T(8,128)(2,1)}, u32[]{:S(2)}) copy-start(bf16[3,512,256]{2,1,0:T(8,128)(2,1)} %param.20) | copy-start | bytes 2359300
  12.4 3.1 copy-start.26
  19.4 4.1 %copy-start.13 = (bf16[256,512]{1,0:T(8,128)(2,1)S(1)}, bf16[256,512]{1,0:T(8,128)(2,1)}, u32[]{:S(2)}) copy-start(bf16[256,512]{1,0:T(8,128)(2,1)} %param.23) | copy-start | bytes 786436
  24.2 25.7 %copy-start.1 = (bf16[196,512]{1,0:T(8,128)(2,1)S(1)}, bf16[196,512]{1,0:T(8,128)(2,1)}, u32[]{:S(2)}) copy-start(bf16[196,512]{1,0:T(8,128)(2,1)} %param.17) | copy-start | bytes 602116
  25.4 25.7 %copy-start.20 = (f32[512]{0:T(512)S(1)}, f32[512]{0:T(512)}, u32[]{:S(2)}) copy-start(f32[512]{0:T(512)} %param.25) | copy-start | bytes 6148
  25.4 25.7 %copy-start.28 = (f32[512]{0:T(512)S(1)}, f32[512]{0:T(512)}, u32[]{:S(2)}) copy-start(f32[512]{0:T(512)} %param.26) | copy-start | bytes 6148
  25.4 25.7 %copy-start.33 = (f32[1024]{0:T(1024)S(1)}, f32[1024]{0:T(1024)}, u32[]{:S(2)}) copy-start(f32[1024]{0:T(1024)} %param.28) | copy-start | bytes 12292
  25.4 51.5 %all-reduce.9.cloned.1.call-start = ((), (), s32[]{:S(2)}) async-start(), calls=%async_computation.1 | async-start | bytes 819200 | tf_op jit(solution)/shard_map/psum | solution.py:145
  57.1 72.1 %all-reduce.11.cloned.1.call-start = ((), (), s32[]{:S(2)}) async-start(), calls=%async_computation.2 | async-start | bytes 819200 | tf_op jit(solution)/shard_map/psum | solution.py:176
  66.0 12.7 %copy-start.35 = (f32[512]{0:T(512)S(1)}, f32[512]{0:T(512)}, u32[]{:S(2)}) copy-start(f32[512]{0:T(512)} %param.30) | copy-start | bytes 6148
  81.5 3.6 copy-start.14
  93.6 2.9 copy-start.3
  109.4 239.9 %all-reduce.13.cloned.1.call-start = ((), (), s32[]{:S(2)}) async-start(), calls=%async_computation.3 | async-start | bytes 12582912 | tf_op jit(solution)/shard_map/psum | solution.py:194
  112.9 16.3 %copy-start.22 = (f32[196]{0:T(256)S(1)}, f32[196]{0:T(256)}, u32[]{:S(2)}) copy-start(f32[196]{0:T(256)} %copy-done.21) | copy-start | bytes 2356
  112.9 16.3 %copy-start.23 = (f32[512]{0:T(512)S(1)}, f32[512]{0:T(512)}, u32[]{:S(2)}) copy-start(f32[512]{0:T(512)} %param.18) | copy-start | bytes 6148
  112.9 16.3 %copy-start.25 = (f32[196]{0:T(256)S(1)}, f32[196]{0:T(256)}, u32[]{:S(2)}) copy-start(f32[196]{0:T(256)} %copy-done.24) | copy-start | bytes 2356
  112.9 17.6 %copy-start.29 = (f32[512]{0:T(512)S(1)}, f32[512]{0:T(512)}, u32[]{:S(2)}) copy-start(f32[512]{0:T(512)} %get-tuple-element.15) | copy-start | bytes 6148
  112.9 17.6 %copy-start.30 = (f32[512]{0:T(512)S(1)}, f32[512]{0:T(512)}, u32[]{:S(2)}) copy-start(f32[512]{0:T(512)} %get-tuple-element.21) | copy-start | bytes 6148
  112.9 17.6 %copy-start.31 = (f32[512]{0:T(512)S(1)}, f32[512]{0:T(512)}, u32[]{:S(2)}) copy-start(f32[512]{0:T(512)} %get-tuple-element.36) | copy-start | bytes 6148
  112.9 17.6 %copy-start.32 = (f32[512]{0:T(512)S(1)}, f32[512]{0:T(512)}, u32[]{:S(2)}) copy-start(f32[512]{0:T(512)} %get-tuple-element.45) | copy-start | bytes 6148
  112.9 17.6 %copy-start.34 = (f32[1024]{0:T(1024)S(1)}, f32[1024]{0:T(1024)}, u32[]{:S(2)}) copy-start(f32[1024]{0:T(1024)} %get-tuple-element.56) | copy-start | bytes 12292
  349.3 3.6 copy-start.5
  (16 other events, 26.2 us)
Sparse Core Ops, SparseCore 0:
  25.5 21.1 all-reduce.6
  57.2 19.6 all-reduce.8
  109.5 19.6 all-reduce.10
  136.6 212.6 all-reduce.12
